TPU v7x, 256 devices: a whole 4x4x8 slice. The times are simulated.
256 devices in a mesh: pb: 8 (over x, y_lo), ka: 4 (over y_hi, core), ha: 8 (over z).
Axes of the slice: x: 4, y: 4 (y_hi: 2, y_lo: 2; y = y_hi * 2 + y_lo), z: 8, core: 2. Of those that a mesh axis runs over, the one named last changes fastest.
Arguments:
- queries: bfloat16 [4096, 64, 128], P(('pb', 'ka'), 'ha'), may hold values from -8 to 8
- keys: bfloat16 [4096, 8, 128], P(('pb', 'ka'), 'ha'), may hold values from -4.5 to 4.5
- values: bfloat16 [4096, 8, 128], P(('pb', 'ka'), 'ha'), may hold values from -12 to 12
- out_grad: bfloat16 [4096, 64, 128], P(('pb', 'ka'), 'ha'), may hold values from -6 to 6
Outputs:
- attended: bfloat16 [4096, 64, 128], P(('pb', 'ka'), 'ha')
- query_grad: bfloat16 [4096, 64, 128], P(('pb', 'ka'), 'ha')
- key_grad: bfloat16 [4096, 8, 128], P(('pb', 'ka'), 'ha')
- value_grad: bfloat16 [4096, 8, 128], P(('pb', 'ka'), 'ha')
All inputs are finite; a program needn't handle non-finite values.
Results may differ from a plain program's by a relative error of at most 0.0097.
Values may be sent and summed in bfloat16 or wider, within the bound.
No kernel may reach another device: no remote copies, remote signals or barrier semaphores. Data moves between devices by JAX's collectives and lax.ppermute only.
A program may use at most 128 MiB of HBM per device.

v0:
```python
import math
import jax
import jax.numpy as jnp
from jax import lax
from jax.sharding import PartitionSpec as P

HEAD_DIM = 128
GROUP = 8


def merged(value, axis, join):
    pieces = jax.tree.map(lambda part: lax.all_gather(part, axis), value)
    head = jax.tree.map(lambda part: part[0], pieces)
    tail = jax.tree.map(lambda part: part[1:], pieces)
    total, _ = lax.scan(lambda total, section: (join(total, section), None), head, tail)
    return total


def combine_partials(earlier, second):
    earlier_max, earlier_total, earlier_sum = earlier
    second_max, second_total, second_sum = second
    joined = jnp.maximum(earlier_max, second_max)
    earlier_factor = jnp.exp(earlier_max - joined)
    second_factor = jnp.exp(second_max - joined)
    merged_total = earlier_total * earlier_factor + second_total * second_factor
    merged_sum = earlier_sum * earlier_factor[..., None] + second_sum * second_factor[..., None]
    return (joined, merged_total, merged_sum)


def make_absorb(grouped, scaling, running, pieces):
    run_max, run_total, run_sum = running
    key_piece, value_piece = pieces
    scores = (
        jnp.einsum("qhgd,khd->hgqk", grouped, key_piece, preferred_element_type=jnp.float32)
        * scaling
    )
    new_max = jnp.max(scores, axis=-1)
    factor = jnp.exp(run_max - new_max)
    weights = jnp.exp(scores - new_max[..., None])
    run_total = run_total * factor + jnp.sum(weights, axis=-1)
    run_sum = run_sum * factor[..., None] + jnp.einsum(
        "hgqk,khd->hgqd",
        weights,
        value_piece.astype(jnp.float32),
        preferred_element_type=jnp.float32,
        precision=lax.Precision.HIGHEST,
    )
    return (new_max, run_total, run_sum)


def start_stats(kv_count, query_total):
    stat_shape = (kv_count, GROUP, query_total)
    return (
        jnp.full(stat_shape, -jnp.inf, jnp.float32),
        jnp.zeros(stat_shape, jnp.float32),
        jnp.zeros(stat_shape + (HEAD_DIM,), jnp.float32),
    )


def backward_blocks(query_heads, grad_heads, log_total, row_dots, key_rows, value_rows, scaling):
    key_total = key_rows.shape[0]
    block_width = math.gcd(key_total, 512)

    def visit_block(grad_running, position):
        first_row = position * block_width
        key_block = lax.dynamic_slice_in_dim(key_rows, first_row, block_width, 0)
        value_block = lax.dynamic_slice_in_dim(value_rows, first_row, block_width, 0)
        scores = (
            jnp.einsum("qhgd,khd->hgqk", query_heads, key_block, preferred_element_type=jnp.float32)
            * scaling
        )
        probs = jnp.exp(scores - log_total[..., None])
        value_part = jnp.einsum(
            "hgqk,qhgd->khd",
            probs.astype(jnp.bfloat16),
            grad_heads,
            preferred_element_type=jnp.float32,
        )
        grad_probs = jnp.einsum(
            "qhgd,khd->hgqk", grad_heads, value_block, preferred_element_type=jnp.float32
        )
        grad_scores = (scaling * probs * (grad_probs - row_dots[..., None])).astype(jnp.bfloat16)
        grad_running = grad_running + jnp.einsum(
            "hgqk,khd->qhgd", grad_scores, key_block, preferred_element_type=jnp.float32
        )
        key_part = jnp.einsum(
            "hgqk,qhgd->khd", grad_scores, query_heads, preferred_element_type=jnp.float32
        )
        return (grad_running, (key_part, value_part))

    initial = jnp.zeros(query_heads.shape, jnp.float32)
    block_count = key_total // block_width
    grad_query, (key_parts, value_parts) = lax.scan(
        visit_block, initial, jnp.arange(block_count, dtype=jnp.int32)
    )
    tail_shape = key_rows.shape
    return (grad_query, key_parts.reshape(tail_shape), value_parts.reshape(tail_shape))


def on_device(queries, keys, values, out_grad):
    local_rows = queries.shape[0]
    head_count = queries.shape[1]
    kv_count = keys.shape[1]
    scaling = HEAD_DIM ** (-0.5)
    own_queries = queries.reshape(local_rows, kv_count, GROUP, HEAD_DIM)
    block_queries = lax.all_gather(queries, "ka", axis=0, tiled=True)
    query_total = block_queries.shape[0]
    grouped = block_queries.reshape(query_total, kv_count, GROUP, HEAD_DIM)
    local_parts = make_absorb(
        grouped,
        scaling,
        start_stats(kv_count, query_total),
        (
            lax.all_gather(keys, "pb", axis=0, tiled=True),
            lax.all_gather(values, "pb", axis=0, tiled=True),
        ),
    )
    whole_max, whole_total, whole_sum = merged(local_parts, "ka", combine_partials)
    first_row = lax.axis_index("ka") * local_rows
    own_max = lax.dynamic_slice_in_dim(whole_max, first_row, local_rows, 2)
    own_total = lax.dynamic_slice_in_dim(whole_total, first_row, local_rows, 2)
    own_sum = lax.dynamic_slice_in_dim(whole_sum, first_row, local_rows, 2)
    exact_out = own_sum / own_total[..., None]
    output_heads = exact_out.astype(jnp.bfloat16)
    log_total = own_max + jnp.log(own_total)
    attended = jnp.transpose(output_heads, (2, 0, 1, 3)).reshape(local_rows, head_count, HEAD_DIM)
    grad_heads = out_grad.reshape(local_rows, kv_count, GROUP, HEAD_DIM)
    row_dots = jnp.einsum(
        "hgqd,qhgd->hgq",
        exact_out,
        grad_heads.astype(jnp.float32),
        preferred_element_type=jnp.float32,
    )
    wide_key, wide_value = (
        lax.all_gather(keys, ("pb", "ka"), axis=0, tiled=True),
        lax.all_gather(values, ("pb", "ka"), axis=0, tiled=True),
    )
    grad_query, key_terms, value_terms = backward_blocks(
        own_queries, grad_heads, log_total, row_dots, wide_key, wide_value, scaling
    )
    grad_key, grad_value = (
        lax.psum_scatter(key_terms, ("pb", "ka"), scatter_dimension=0, tiled=True),
        lax.psum_scatter(value_terms, ("pb", "ka"), scatter_dimension=0, tiled=True),
    )
    query_grad = grad_query.astype(jnp.bfloat16).reshape(local_rows, head_count, HEAD_DIM)
    return (attended, query_grad, grad_key.astype(jnp.bfloat16), grad_value.astype(jnp.bfloat16))


def solution(mesh):
    return jax.shard_map(
        on_device,
        mesh=mesh,
        in_specs=(
            P(("pb", "ka"), "ha", None),
            P(("pb", "ka"), "ha", None),
            P(("pb", "ka"), "ha", None),
            P(("pb", "ka"), "ha", None),
        ),
        out_specs=(
            P(("pb", "ka"), "ha", None),
            P(("pb", "ka"), "ha", None),
            P(("pb", "ka"), "ha", None),
            P(("pb", "ka"), "ha", None),
        ),
        check_vma=False,
    )
```

profile of v0, /device:TPU:32, one launch (start us, length us, event | category | flops | bytes accessed | tf_op | source)
XLA Modules:
  0.0 639.3 jit_solution(16966723260642444875)
XLA Ops:
  7.2 1.7 copy.52
  9.0 28.9 %all_gather.31 = bf16[1024,1,128]{2,0,1:T(8,128)(2,1)S(1)} all-gather(bf16[128,1,128]{2,0,1:T(8,128)(2,1)} %param.9), channel_id=1, replica_groups=mesh['pb'=8,'ka'=4,'ha'=8] {'pb'}, dimensions={0}, use_global_device_ids=true | all-gather | bytes 294912 | tf_op jit(solution)/shard_map/all_gather | solution.py:114
  37.9 28.7 %all_gather.36 = bf16[1024,1,128]{2,0,1:T(8,128)(2,1)S(1)} all-gather(bf16[128,1,128]{2,0,1:T(8,128)(2,1)} %param.10), channel_id=1, replica_groups=mesh['pb'=8,'ka'=4,'ha'=8] {'pb'}, dimensions={0}, use_global_device_ids=true | all-gather | bytes 294912 | tf_op jit(solution)/shard_map/all_gather | solution.py:115
  66.6 9.3 %bitcast_reduce_fusion = (f32[8,512]{1,0:T(8,128)S(1)}, f32[1024,512,8]{1,0,2:T(8,128)}) fusion(bf16[512,8,128]{2,0,1:T(8,128)(2,1)} %all-gather.7.cloned.1.call-done, bf16[1024,1,128]{2,0,1:T(8,128)(2,1)S(1)} %all_gather.31), kind=kOutput, calls=%fused_computation.44 | convolution fusion | flops 1082126336 | bytes 18104320 | tf_op jit(solution)/shard_map/qhgd,khd->hgqk/dot_general | solution.py:34
  75.9 8.5 %fusion.36 = f32[8,512]{1,0:T(8,128)S(1)} fusion(f32[1024,512,8]{1,0,2:T(8,128)} %get-tuple-element.212, f32[8,512]{1,0:T(8,128)S(1)} %get-tuple-element.211), kind=kLoop, calls=%fused_computation.46 | loop fusion | flops 12578816 | bytes 16809984 | tf_op jit(solution)/shard_map/reduce_sum | solution.py:40
  84.4 18.9 %fusion.39 = f32[8,512,128]{2,1,0:T(8,128)} fusion(f32[1024,512,8]{1,0,2:T(8,128)} %get-tuple-element.212, f32[8,512]{1,0:T(8,128)S(1)} %get-tuple-element.211, f32[8,512]{1,0:T(8,128)S(1)} %get-tuple-element.209, bf16[1024,1,128]{2,0,1:T(8,128)(2,1)S(1)} %all_gather.36), kind=kOutput, calls=%fused_computation.50 | convolution fusion | flops 6451363840 | bytes 19169280 | tf_op jit(solution)/shard_map/hgqk,khd->hgqd/dot_general | solution.py:41
  104.8 6.7 %all_gather.35 = f32[4,1,8,512]{3,2,1,0:T(8,128)S(1)} all-gather(f32[1,1,8,512]{3,2,1,0:T(8,128)S(1)} %get-tuple-element.210), channel_id=1, replica_groups=mesh['pb'=8,'ka'=4,'ha'=8] {'ka'}, dimensions={0}, use_global_device_ids=true | all-gather | bytes 81920 | tf_op jit(solution)/shard_map/all_gather | solution.py:12
  111.5 6.8 %all-gather = f32[32,512]{1,0:T(8,128)S(1)} all-gather(f32[8,512]{1,0:T(8,128)S(1)} %get-tuple-element.211), channel_id=2, replica_groups=mesh['pb'=8,'ka'=4,'ha'=8] {'ka'}, dimensions={0}, use_global_device_ids=true | all-gather | bytes 81920 | tf_op jit(solution)/shard_map/all_gather | solution.py:12
  118.3 52.3 %all-gather.13.cloned.1.call-done = f32[32,512,128]{2,1,0:T(8,128)} async-done(((f32[8,512,128]{2,1,0:T(8,128)}), f32[32,512,128]{2,1,0:T(8,128)}) %all-gather.13.cloned.1.call-update) | async-done | bytes 8388624 | tf_op jit(solution)/shard_map/all_gather | solution.py:12
  170.6 6.1 slice.33
  176.7 1.7 slice_bitcast_fusion
  178.4 8.6 %while.29 = (s32[]{:T(128)}, f32[1,8,512]{2,1,0:T(8,128)S(1)}, f32[1,8,512]{2,1,0:T(8,128)S(1)}, f32[1,8,512,128]{3,2,1,0:T(8,128)S(1)}, f32[3,1,8,512]{3,2,1,0:...) while((s32[]{:T(128)}, f32[1,8,512]{2,1,0:T(8,128)S(1)}, ...), condition=%wide.region_3.4_spmd, body=%wide.region_2.3_spmd.sunk | while | flops 1601538 | bytes 6537313 | solution.py:15
  178.7 2.7 fusion.70
  181.5 2.7 fusion.70
  184.3 2.7 fusion.70
  187.0 2.5 copy.33
  191.2 38.9 %all-gather.11.cloned.1.call-done = bf16[4096,1,128]{2,0,1:T(8,128)(2,1)} async-done(((bf16[128,1,128]{2,0,1:T(8,128)(2,1)}), bf16[4096,1,128]{2,0,1:T(8,128)(2,1)}) %all-gather.11.cloned.1.call-update) | async-done | bytes 1048592 | tf_op jit(solution)/shard_map/all_gather | solution.py:136
  230.1 59.3 %all-gather.9.cloned.1.call-done = bf16[4096,1,128]{2,0,1:T(8,128)(2,1)} async-done(((bf16[128,1,128]{2,0,1:T(8,128)(2,1)}), bf16[4096,1,128]{2,0,1:T(8,128)(2,1)}) %all-gather.9.cloned.1.call-update) | async-done | bytes 1048592 | tf_op jit(solution)/shard_map/all_gather | solution.py:135
  289.5 63.0 %while.30 = (s32[]{:T(128)}, f32[128,1,8,128]{0,3,2,1:T(8,128)S(1)}, f32[8,512,1,128]{3,1,2,0:T(8,128)}, f32[8,512,1,128]{3,1,2,0:T(8,128)}, s32[8]{0:T(128)S(1)...) while((s32[]{:T(128)}, ...), condition=%wide.region_5.6_spmd.clone, body=%wide.region_4.5_spmd.clone.sunk | while | flops 676069376 | bytes 12465373 | solution.py:93
  292.0 1.6 fusion.82
  299.9 1.6 fusion.82
  307.8 1.6 fusion.82
  315.7 1.6 fusion.82
  323.5 1.6 fusion.82
  331.4 1.6 fusion.82
  339.3 1.6 fusion.82
  347.2 1.6 fusion.82
  354.0 2.0 convert_bitcast_fusion.1
  356.0 136.3 %reduce-scatter.3.cloned.1.call-done = f32[128,1,128]{2,0,1:T(8,128)} async-done(((f32[4096,1,128]{2,0,1:T(8,128)}), f32[128,1,128]{2,0,1:T(8,128)}) %reduce-scatter.3.cloned.1.call-update) | async-done | bytes 65552 | tf_op jit(solution)/shard_map/reduce_scatter | solution.py:142
  492.3 1.5 convert_element_type.22
  493.7 137.3 %reduce-scatter.5.cloned.1.call-done = f32[128,1,128]{2,0,1:T(8,128)} async-done(((f32[4096,1,128]{2,0,1:T(8,128)}), f32[128,1,128]{2,0,1:T(8,128)}) %reduce-scatter.5.cloned.1.call-update) | async-done | bytes 65552 | tf_op jit(solution)/shard_map/reduce_scatter | solution.py:143
  631.0 1.5 convert_element_type.23
  (81 shorter events, 49.3 us)
Async XLA Ops:
  7.2 59.4 %all-gather.7.cloned.1.call-start = ((), (), s32[]{:S(2)}) async-start(), calls=%async_computation.2 | async-start | bytes 1310720 | tf_op jit(solution)/shard_map/all_gather | solution.py:106
  8.9 161.7 %all-gather.13.cloned.1.call-start = ((), (), s32[]{:S(2)}) async-start(), calls=%async_computation.7 | async-start | bytes 10485760 | tf_op jit(solution)/shard_map/all_gather | solution.py:12
  103.3 1.4 copy-start.1
  103.3 126.8 %all-gather.11.cloned.1.call-start = ((), (), s32[]{:S(2)}) async-start(), calls=%async_computation.4 | async-start | bytes 1081344 | tf_op jit(solution)/shard_map/all_gather | solution.py:136
  104.1 185.4 %all-gather.9.cloned.1.call-start = ((), (), s32[]{:S(2)}) async-start(), calls=%async_computation.3 | async-start | bytes 1081344 | tf_op jit(solution)/shard_map/all_gather | solution.py:135
  104.7 387.6 %reduce-scatter.3.cloned.1.call-start = ((), (), s32[]{:S(2)}) async-start(), calls=%async_computation.5 | async-start | bytes 2162688 | tf_op jit(solution)/shard_map/reduce_scatter | solution.py:142
  187.0 102.4 %copy-start = (bf16[128,8,128]{2,0,1:T(8,128)(2,1)S(1)}, bf16[128,8,128]{2,0,1:T(8,128)(2,1)}, u32[]{:S(2)}) copy-start(bf16[128,8,128]{2,0,1:T(8,128)(2,1)} %copy.52) | copy-start | bytes 786436
  352.5 278.5 %reduce-scatter.5.cloned.1.call-start = ((), (), s32[]{:S(2)}) async-start(), calls=%async_computation.6 | async-start | bytes 2162688 | tf_op jit(solution)/shard_map/reduce_scatter | solution.py:143
Sparse Core Ops, SparseCore 0:
  10.4 27.1 all-gather.6
  103.5 67.0 all-gather.12
  172.5 57.5 all-gather.10
  231.8 57.5 all-gather.8
  352.6 139.5 reduce-scatter.2
  494.6 136.3 reduce-scatter.4
where the time goes:
time: 640 us; the launch traced here: 639 us
  waiting for transfers between devices  426 us (67%)
  matrix products  81 us (13%)
  blocking collectives  71.1 us (11%)
  other arithmetic  23 us (4%)
  local copies, waits for them, and re-layouts  17.9 us (3%)
  between operations  14.2 us (2%)
    reduce_scatter x1, waiting for transfers between devices, on_device(): lax.psum_scatter(value_terms, ('pb', 'ka'), scatter_dimension=0, tiled=True)  137 us
    reduce_scatter x1, waiting for transfers between devices, on_device(): lax.psum_scatter(key_terms, ('pb', 'ka'), scatter_dimension=0, tiled=True)  136 us
    all_gather x1, waiting for transfers between devices, on_device(): lax.all_gather(keys, ('pb', 'ka'), axis=0, tiled=True)  59.3 us
    all_gather x1, waiting for transfers between devices, merged(): pieces = jax.tree.map(lambda part: lax.all_gather(part, axis), value)  52.3 us
    all_gather x1, waiting for transfers between devices, on_device(): lax.all_gather(values, ('pb', 'ka'), axis=0, tiled=True)  38.9 us
    all_gather x1, blocking collectives, on_device(): lax.all_gather(keys, 'pb', axis=0, tiled=True)  28.9 us
    all_gather x1, blocking collectives, on_device(): lax.all_gather(values, 'pb', axis=0, tiled=True)  28.7 us
    dot_general x1, matrix products, make_absorb(): jnp.einsum('hgqk,khd->hgqd', weights, value_piece.astype(jnp.float32), pr...  18.9 us
  transfers between devices with their start and end apart: 6, of which 5 were waited for; matrix products, arithmetic and copies ran while one was open for 4% of the time, Pallas kernels for 0%

commit v1 on v0

--- a/solution.py
+++ b/solution.py
@@ -6,6 +6,13 @@
 
 HEAD_DIM = 128
 GROUP = 8
+
+
+def all_by_exchange(value, name, dim):
+    size = lax.axis_size(name)
+    blocks = jnp.stack([value for _ in range(size)])
+    blocks = lax.all_to_all(blocks, name, split_axis=0, concat_axis=0)
+    return jnp.concatenate(blocks, axis=dim)
 
 
 def merged(value, axis, join):
@@ -132,7 +139,7 @@
         preferred_element_type=jnp.float32,
     )
     wide_key, wide_value = (
-        lax.all_gather(keys, ("pb", "ka"), axis=0, tiled=True),
+        all_by_exchange(keys, ("pb", "ka"), 0),
         lax.all_gather(values, ("pb", "ka"), axis=0, tiled=True),
     )
     grad_query, key_terms, value_terms = backward_blocks(

time: 640 us -> 586 us (0.916)
  waiting for transfers between devices: 426 us -> 353 us
  blocking collectives: 71.1 us -> 81.6 us
  starting transfers between devices: 0.24 us -> 6.96 us
    all_gather x1 -> x0, waiting for transfers between devices: 59.3 us -> none  [on_device(): lax.all_gather(keys, ('pb', 'ka'), axis=0, tiled=True)]
    all_gather x1, waiting for transfers between devices: 52.3 us -> 38.8 us  [merged(): pieces = jax.tree.map(lambda part: lax.all_gather(part, axis), value)]
    all_gather x2, blocking collectives: 13.5 us -> 24 us  [merged(): pieces = jax.tree.map(lambda part: lax.all_gather(part, axis), value)]
    all_to_all x0 -> x1, starting transfers between devices: none -> 6.76 us  [all_by_exchange(): blocks = lax.all_to_all(blocks, name, split_axis=0, concat_axis=0)]
  transfers between devices with their start and end apart: 6 -> 6, of which waited for: 5 -> 4; matrix products, arithmetic and copies ran while one was open for 4% -> 4% of each run, Pallas kernels for 0% -> 0%
where the time goes in v1:
time: 586 us; the launch traced here: 585 us
  waiting for transfers between devices  353 us (60%)
  blocking collectives  81.6 us (14%)
  matrix products  81 us (14%)
  other arithmetic  23 us (4%)
  local copies, waits for them, and re-layouts  19.8 us (3%)
  between operations  13.9 us (2%)
  starting transfers between devices  6.96 us (1%)
  loops' own time  5.88 us (1%)
    reduce_scatter x1, waiting for transfers between devices, on_device(): lax.psum_scatter(value_terms, ('pb', 'ka'), scatter_dimension=0, tiled=True)  137 us
    reduce_scatter x1, waiting for transfers between devices, on_device(): lax.psum_scatter(key_terms, ('pb', 'ka'), scatter_dimension=0, tiled=True)  136 us
    all_gather x1, waiting for transfers between devices, on_device(): lax.all_gather(values, ('pb', 'ka'), axis=0, tiled=True)  39.9 us
    all_gather x1, waiting for transfers between devices, merged(): pieces = jax.tree.map(lambda part: lax.all_gather(part, axis), value)  38.8 us
    all_gather x1, blocking collectives, on_device(): lax.all_gather(keys, 'pb', axis=0, tiled=True)  28.9 us
    all_gather x1, blocking collectives, on_device(): lax.all_gather(values, 'pb', axis=0, tiled=True)  28.7 us
    all_gather x2, blocking collectives, merged(): pieces = jax.tree.map(lambda part: lax.all_gather(part, axis), value)  24 us
    dot_general x1, matrix products, make_absorb(): jnp.einsum('hgqk,khd->hgqd', weights, value_piece.astype(jnp.float32), pr...  18.9 us
  transfers between devices with their start and end apart: 6, of which 4 were waited for; matrix products, arithmetic and copies ran while one was open for 4% of the time, Pallas kernels for 0%

profile of v1, /device:TPU:32, one launch (start us, length us, event | category | flops | bytes accessed | tf_op | source)
XLA Modules:
  0.0 585.1 jit_solution(3431825439154348425)
XLA Ops:
  7.2 1.7 copy.52
  9.0 28.9 %all_gather.28 = bf16[1024,1,128]{2,0,1:T(8,128)(2,1)S(1)} all-gather(bf16[128,1,128]{2,0,1:T(8,128)(2,1)} %param.9), channel_id=1, replica_groups=mesh['pb'=8,'ka'=4,'ha'=8] {'pb'}, dimensions={0}, use_global_device_ids=true | all-gather | bytes 294912 | tf_op jit(solution)/shard_map/all_gather | solution.py:121
  37.9 28.7 %all_gather.33 = bf16[1024,1,128]{2,0,1:T(8,128)(2,1)S(1)} all-gather(bf16[128,1,128]{2,0,1:T(8,128)(2,1)} %param.10), channel_id=1, replica_groups=mesh['pb'=8,'ka'=4,'ha'=8] {'pb'}, dimensions={0}, use_global_device_ids=true | all-gather | bytes 294912 | tf_op jit(solution)/shard_map/all_gather | solution.py:122
  66.6 9.3 %bitcast_reduce_fusion = (f32[8,512]{1,0:T(8,128)S(1)}, f32[1024,512,8]{1,0,2:T(8,128)}) fusion(bf16[512,8,128]{2,0,1:T(8,128)(2,1)} %all-gather.6.cloned.1.call-done, bf16[1024,1,128]{2,0,1:T(8,128)(2,1)S(1)} %all_gather.28), kind=kOutput, calls=%fused_computation.44 | convolution fusion | flops 1082126336 | bytes 18104320 | tf_op jit(solution)/shard_map/qhgd,khd->hgqk/dot_general | solution.py:41
  75.9 8.5 %fusion.36 = f32[8,512]{1,0:T(8,128)S(1)} fusion(f32[1024,512,8]{1,0,2:T(8,128)} %get-tuple-element.212, f32[8,512]{1,0:T(8,128)S(1)} %get-tuple-element.211), kind=kLoop, calls=%fused_computation.46 | loop fusion | flops 12578816 | bytes 16809984 | tf_op jit(solution)/shard_map/reduce_sum | solution.py:47
  84.4 18.9 %fusion.39 = f32[8,512,128]{2,1,0:T(8,128)} fusion(f32[1024,512,8]{1,0,2:T(8,128)} %get-tuple-element.212, f32[8,512]{1,0:T(8,128)S(1)} %get-tuple-element.211, f32[8,512]{1,0:T(8,128)S(1)} %get-tuple-element.209, bf16[1024,1,128]{2,0,1:T(8,128)(2,1)S(1)} %all_gather.33), kind=kOutput, calls=%fused_computation.50 | convolution fusion | flops 6451363840 | bytes 19169280 | tf_op jit(solution)/shard_map/hgqk,khd->hgqd/dot_general | solution.py:48
  105.3 6.8 %all-to-all-start = ((bf16[32,128,1,128]{3,1,2,0:T(8,128)(2,1)}), bf16[32,128,1,128]{3,1,2,0:T(8,128)(2,1)}, u32[]{:S(2)}, u32[]{:S(2)}) async-start(bf16[32,128,1,128]{3,1,2,0:T(8,128)(2,1)} %stack.2), calls=%async_computation | async-start | bytes 2097152 | tf_op jit(solution)/shard_map/all_to_all | solution.py:14
  112.9 16.8 %all_gather.32 = f32[4,1,8,512]{3,2,1,0:T(8,128)S(1)} all-gather(f32[1,1,8,512]{3,2,1,0:T(8,128)S(1)} %get-tuple-element.210), channel_id=1, replica_groups=mesh['pb'=8,'ka'=4,'ha'=8] {'ka'}, dimensions={0}, use_global_device_ids=true | all-gather | bytes 81920 | tf_op jit(solution)/shard_map/all_gather | solution.py:19
  129.8 7.1 %all-gather = f32[32,512]{1,0:T(8,128)S(1)} all-gather(f32[8,512]{1,0:T(8,128)S(1)} %get-tuple-element.211), channel_id=2, replica_groups=mesh['pb'=8,'ka'=4,'ha'=8] {'ka'}, dimensions={0}, use_global_device_ids=true | all-gather | bytes 81920 | tf_op jit(solution)/shard_map/all_gather | solution.py:19
  136.9 38.8 %all-gather.10.cloned.1.call-done = f32[32,512,128]{2,1,0:T(8,128)} async-done(((f32[8,512,128]{2,1,0:T(8,128)}), f32[32,512,128]{2,1,0:T(8,128)}) %all-gather.10.cloned.1.call-update) | async-done | bytes 8388624 | tf_op jit(solution)/shard_map/all_gather | solution.py:19
  175.7 6.1 %slice.33 = f32[24,512,128]{2,1,0:T(8,128)} slice(f32[32,512,128]{2,1,0:T(8,128)} %all-gather.10.cloned.1.call-done), slice={[8:32], [0:512], [0:128]} | slice | bytes 12582912 | tf_op jit(solution)/shard_map/slice | solution.py:21
  181.8 1.7 slice_bitcast_fusion
  183.5 8.6 %while.29 = (s32[]{:T(128)}, f32[1,8,512]{2,1,0:T(8,128)S(1)}, f32[1,8,512]{2,1,0:T(8,128)S(1)}, f32[1,8,512,128]{3,2,1,0:T(8,128)S(1)}, f32[3,1,8,512]{3,2,1,0:...) while((s32[]{:T(128)}, f32[1,8,512]{2,1,0:T(8,128)S(1)}, ...), condition=%wide.region_3.4_spmd, body=%wide.region_2.3_spmd.sunk | while | flops 1601538 | bytes 6537313 | solution.py:22
  183.8 2.7 fusion.70
  186.6 2.7 fusion.70
  189.4 2.7 fusion.70
  192.1 2.5 copy.33
  196.2 39.9 %all-gather.8.cloned.1.call-done = bf16[4096,1,128]{2,0,1:T(8,128)(2,1)} async-done(((bf16[128,1,128]{2,0,1:T(8,128)(2,1)}), bf16[4096,1,128]{2,0,1:T(8,128)(2,1)}) %all-gather.8.cloned.1.call-update) | async-done | bytes 1048592 | tf_op jit(solution)/shard_map/all_gather | solution.py:143
  236.1 63.0 %while.30 = (s32[]{:T(128)}, f32[128,1,8,128]{0,3,2,1:T(8,128)S(1)}, f32[8,512,1,128]{3,1,2,0:T(8,128)}, f32[8,512,1,128]{3,1,2,0:T(8,128)}, s32[8]{0:T(128)S(1)...) while((s32[]{:T(128)}, ...), condition=%wide.region_5.6_spmd.clone, body=%wide.region_4.5_spmd.clone.sunk | while | flops 676069376 | bytes 12465373 | solution.py:100
  238.7 1.6 fusion.82
  246.6 1.6 fusion.82
  254.5 1.6 fusion.82
  262.3 1.6 fusion.82
  270.2 1.6 fusion.82
  278.1 1.6 fusion.82
  286.0 1.6 fusion.82
  293.9 1.6 fusion.82
  300.7 2.0 convert_bitcast_fusion.1
  302.7 135.9 %reduce-scatter.3.cloned.1.call-done = f32[128,1,128]{2,0,1:T(8,128)} async-done(((f32[4096,1,128]{2,0,1:T(8,128)}), f32[128,1,128]{2,0,1:T(8,128)}) %reduce-scatter.3.cloned.1.call-update) | async-done | bytes 65552 | tf_op jit(solution)/shard_map/reduce_scatter | solution.py:149
  438.6 1.5 convert_element_type.22
  440.0 137.1 %reduce-scatter.5.cloned.1.call-done = f32[128,1,128]{2,0,1:T(8,128)} async-done(((f32[4096,1,128]{2,0,1:T(8,128)}), f32[128,1,128]{2,0,1:T(8,128)}) %reduce-scatter.5.cloned.1.call-update) | async-done | bytes 65552 | tf_op jit(solution)/shard_map/reduce_scatter | solution.py:150
  577.2 1.5 convert_element_type.23
  (83 shorter events, 50.7 us)
Async XLA Ops:
  7.2 59.4 %all-gather.6.cloned.1.call-start = ((), (), s32[]{:S(2)}) async-start(), calls=%async_computation.3 | async-start | bytes 1310720 | tf_op jit(solution)/shard_map/all_gather | solution.py:113
  8.9 166.8 %all-gather.10.cloned.1.call-start = ((), (), s32[]{:S(2)}) async-start(), calls=%async_computation.7 | async-start | bytes 10485760 | tf_op jit(solution)/shard_map/all_gather | solution.py:19
  103.3 0.8 copy-start.2
  103.3 9.5 %copy-start.1 = (bf16[128,8,128]{2,1,0:T(8,128)(2,1)S(1)}, bf16[128,8,128]{2,1,0:T(8,128)(2,1)}, u32[]{:S(2)}) copy-start(bf16[128,8,128]{2,1,0:T(8,128)(2,1)} %param.11) | copy-start | bytes 786436
  105.3 91.0 %all-to-all-start = ((bf16[32,128,1,128]{3,1,2,0:T(8,128)(2,1)}), bf16[32,128,1,128]{3,1,2,0:T(8,128)(2,1)}, u32[]{:S(2)}, u32[]{:S(2)}) async-start(bf16[32,128,1,128]{3,1,2,0:T(8,128)(2,1)} %stack.2), calls=%async_computation | async-start | bytes 2097152 | tf_op jit(solution)/shard_map/all_to_all | solution.py:14
  112.1 124.1 %all-gather.8.cloned.1.call-start = ((), (), s32[]{:S(2)}) async-start(), calls=%async_computation.4 | async-start | bytes 1081344 | tf_op jit(solution)/shard_map/all_gather | solution.py:143
  112.8 325.8 %reduce-scatter.3.cloned.1.call-start = ((), (), s32[]{:S(2)}) async-start(), calls=%async_computation.5 | async-start | bytes 2162688 | tf_op jit(solution)/shard_map/reduce_scatter | solution.py:149
  192.1 44.0 %copy-start = (bf16[128,8,128]{2,0,1:T(8,128)(2,1)S(1)}, bf16[128,8,128]{2,0,1:T(8,128)(2,1)}, u32[]{:S(2)}) copy-start(bf16[128,8,128]{2,0,1:T(8,128)(2,1)} %copy.52) | copy-start | bytes 786436
  299.2 278.0 %reduce-scatter.5.cloned.1.call-start = ((), (), s32[]{:S(2)}) async-start(), calls=%async_computation.6 | async-start | bytes 2162688 | tf_op jit(solution)/shard_map/reduce_scatter | solution.py:150
Sparse Core Ops, SparseCore 0:
  10.4 27.1 all-gather.5
  103.5 72.1 all-gather.9
  177.6 58.5 all-gather.7
  299.3 139.1 reduce-scatter.2
  440.9 136.1 reduce-scatter.4
